TPU v7x, 256 devices: a whole 4x4x8 slice. The times are simulated.
256 devices in a mesh: rows: 64 (over z, x_hi, y), cols: 4 (over x_lo, core).
Axes of the slice: x: 4 (x_hi: 2, x_lo: 2; x = x_hi * 2 + x_lo), y: 4, z: 8, core: 2. Of those that a mesh axis runs over, the one named last changes fastest.
Arguments:
- cov_panel: float32 [65536, 512], P('rows', 'cols'), may hold values from -12 to 40, as said below
- cov_slab: float32 [65536, 4096], P('rows', 'cols'), may hold values from -6 to 6
- frames: float32 [65536, 256], P('rows'), may hold values from -0.0625 to 0.0625
Outputs:
- updated_slab: float32 [65536, 4096], P('rows', 'cols')
- projected: float32 [256, 4096], P('rows', 'cols')
Inputs may be any that keep to these rules, and one draw needn't show every extreme that they name: `cov_panel`: the rows d1 and d2 restricted to the first 512 columns form a symmetric positive definite matrix.
All inputs are finite; a program needn't handle non-finite values.
Results may differ from a plain program's by a relative error of at most 0.00011.
Values sent between devices are 32-bit elements; how exact they have to be, the bound alone decides.
A program may use at most 64 MiB of HBM per device.

v0:
```python
import functools

import jax
import jax.numpy as jnp
from jax import lax
from jax.experimental import pallas as pl
from jax.experimental.pallas import tpu as pltpu
from jax.sharding import PartitionSpec as P

NZ, NX, NY, NC = 8, 2, 4, 4
NXY = NX * NY
PIV = 16
BLK = 128
MESH = pl.DeviceIdType.MESH
F32, BF16 = jnp.float32, jnp.bfloat16
NN = (((1,), (0,)), ((), ()))
NT = (((1,), (1,)), ((), ()))


def exact(left, right):
    return lax.dot_general(
        left, right, NN, precision=lax.Precision.HIGHEST, preferred_element_type=F32
    )


def halves(x):
    high = x.astype(BF16)
    return high, (x - high.astype(F32)).astype(BF16)


def dot3(left, right, dims):
    (lh, ll), (rh, rl) = left, right
    dot = functools.partial(lax.dot_general, dimension_numbers=dims, preferred_element_type=F32)
    return dot(lh, rh) + (dot(lh, rl) + dot(ll, rh))


def small_inverse(cols):
    row = lax.broadcasted_iota(jnp.int32, (PIV, 128), 0)
    cols = list(cols)
    for j in range(PIV):
        across = [jnp.broadcast_to(col[j : j + 1, :], (PIV, 128)) for col in cols]
        recip = 1.0 / across[j]
        here = row == j
        pivot = jnp.where(here, -1.0, cols[j])
        for k in range(PIV):
            if k != j:
                cols[k] = jnp.where(here, 0.0, cols[k]) - pivot * (across[k] * recip)
        cols[j] = -pivot * recip
    return cols


def block_inverse(parts):
    lane = lax.broadcasted_iota(jnp.int32, (PIV, BLK), 1)
    row = lax.broadcasted_iota(jnp.int32, (PIV, BLK), 0)
    parts = list(parts)
    count = BLK // PIV

    def total(terms):
        sums = terms[:4]
        for i, term in enumerate(terms[4:]):
            sums[i % 4] = sums[i % 4] + term
        return (sums[0] + sums[1]) + (sums[2] + sums[3])

    for m in range(count):
        cols = [
            [
                jnp.broadcast_to(part[:, PIV * m + k : PIV * m + k + 1], (PIV, BLK))
                for k in range(PIV)
            ]
            for part in parts
        ]
        inverse = small_inverse(cols[m])
        inside = (lane >= PIV * m) & (lane < PIV * m + PIV)
        panel = jnp.where(inside, jnp.where(lane - PIV * m == row, 1.0, 0.0), parts[m])
        solved = total(
            [inverse[k] * jnp.broadcast_to(panel[k : k + 1, :], (PIV, BLK)) for k in range(PIV)]
        )
        spread = [jnp.broadcast_to(solved[k : k + 1, :], (PIV, BLK)) for k in range(PIV)]
        for t in range(1, count):
            i = (m + t) % count
            parts[i] = jnp.where(inside, 0.0, parts[i]) - total(
                [cols[i][k] * spread[k] for k in range(PIV)]
            )
        parts[m] = solved
    return jnp.concatenate(parts, axis=0)


def eliminate(mat, k):
    size = mat.shape[0]
    at = pl.multiple_of(k * BLK, BLK)
    parts = [
        mat[pl.ds(pl.multiple_of(at + PIV * i, PIV), PIV), pl.ds(at, BLK)]
        for i in range(BLK // PIV)
    ]
    inverse = block_inverse(parts)
    lane = lax.broadcasted_iota(jnp.int32, (BLK, size), 1) - at
    row = lax.broadcasted_iota(jnp.int32, (BLK, size), 0)
    inside = (lane >= 0) & (lane < BLK)
    panel = jnp.where(inside, jnp.where(lane == row, 1.0, 0.0), mat[pl.ds(at, BLK), :])
    solved = exact(inverse, panel)
    lanes = lax.broadcasted_iota(jnp.int32, (size, size), 1) - at
    cleared = jnp.where((lanes >= 0) & (lanes < BLK), 0.0, mat[...])
    mat[...] = cleared - exact(mat[:, pl.ds(at, BLK)], solved)
    mat[pl.ds(at, BLK), :] = solved


def wait_bytes(ref, sem):
    pltpu.make_async_copy(ref, ref, sem).wait()


def exchange_kernel(
    panel,
    slab,
    frames,
    weights,
    wide,
    proj,
    diag,
    mat,
    owned,
    slab_v,
    frames_v,
    panel_v,
    part,
    part_in,
    line,
    line_in,
    head,
    load_sem,
    send_sem,
    recv_sem,
    ring_send,
    ring_recv,
):
    rows_at, c = lax.axis_index("rows"), lax.axis_index("cols")
    z, xy = rows_at // NXY, lax.rem(rows_at, NXY)
    x, y = xy // NY, lax.rem(xy, NY)

    def place(dz=0, dx=0, dy=0, dc=0):
        z2 = lax.rem(z + dz, NZ)
        x2 = lax.rem(x + dx, NX)
        y2 = lax.rem(y + dy, NY)
        c2 = c
        if dc & 1:
            c2 = c2 + 1 - 2 * lax.rem(c2, 2)
        if dc & 2:
            c2 = lax.rem(c2 + 2, NC)
        return (z2 * NXY + x2 * NY + y2, c2)

    def lanes(col):
        return pl.ds(pl.multiple_of(col * 128, 128), 128)

    def send(src, dst, i, to):
        copy = pltpu.make_async_remote_copy(
            src_ref=src,
            dst_ref=dst,
            send_sem=send_sem.at[i],
            recv_sem=recv_sem.at[i],
            device_id=to,
            device_id_type=MESH,
        )
        copy.start()

    loads = [
        pltpu.make_async_copy(panel, panel_v, load_sem.at[0]),
        pltpu.make_async_copy(frames, frames_v, load_sem.at[1]),
        pltpu.make_async_copy(slab, slab_v, load_sem.at[2]),
        pltpu.make_async_copy(
            panel.at[pl.ds(0, 8), :], diag.at[z, xy, :, lanes(c)], load_sem.at[3]
        ),
        pltpu.make_async_copy(
            panel.at[pl.ds(pl.multiple_of(8 + 16 * c, 8), 16), :],
            owned.at[z, xy, :, lanes(c)],
            load_sem.at[4],
        ),
    ]
    for load in loads:
        load.start()

    line_peers = [dict(dz=d) for d in range(1, NZ)]
    plane_peers = [
        dict(dx=a, dy=b, dc=e) for a in range(NX) for b in range(NY) for e in range(NC) if a or b or e
    ]
    barrier = pltpu.get_barrier_semaphore()
    for peer in line_peers + plane_peers:
        pl.semaphore_signal(barrier, inc=1, device_id=place(**peer), device_id_type=MESH)
    pl.semaphore_wait(barrier, len(line_peers) + len(plane_peers))

    for peer in line_peers:
        send(panel.at[pl.ds(0, 8), :], diag.at[z, xy, :, lanes(c)], 0, place(**peer))
    for e in range(1, NC):
        to = place(dc=e)
        send(
            panel.at[pl.ds(pl.multiple_of(8 + 16 * to[1], 8), 16), :],
            owned.at[z, xy, :, lanes(c)],
            1,
            to,
        )

    loads[0].wait()
    own_wide = pltpu.make_async_copy(panel_v, wide.at[:, lanes(c)], load_sem.at[0])
    own_wide.start()
    loads[1].wait()
    turned = halves(frames_v[...].T)
    shared = dot3(turned, halves(panel_v[...]), NN)
    for g in range(NZ * NXY):
        part[g % NXY, g // NXY, :, 1024:1152] = shared[4 * g : 4 * g + 4, :]
    loads[2].wait()

    def product(i, carry):
        at = pl.multiple_of(i * 256, 256)
        value = dot3(turned, halves(slab_v[:, pl.ds(at, 256)]), NN)
        for g in range(NZ * NXY):
            part[g % NXY, g // NXY, :, pl.ds(at, 256)] = value[4 * g : 4 * g + 4, :]
        return carry

    lax.fori_loop(0, 4, product, 0)

    loads[3].wait()
    wait_bytes(diag.at[pl.ds(0, NZ - 1), xy, :, lanes(c)], recv_sem.at[0])
    same_core = [p for p in plane_peers if not p["dc"] & 1]
    for peer in same_core:
        send(
            diag.at[:, xy, :, lanes(c)], diag.at[:, xy, :, lanes(c)], 2, place(**peer)
        )
    loads[4].wait()
    wait_bytes(owned.at[0, 0, :, pl.ds(0, 384)], recv_sem.at[1])
    plane_only = [p for p in plane_peers if not p["dc"]]
    for peer in plane_only:
        send(owned.at[z, xy], owned.at[z, xy], 3, place(**peer))

    wait_bytes(diag.at[:, pl.ds(0, 5), :, pl.ds(0, 384)], recv_sem.at[2])
    core = lax.rem(c, 2)
    partner = place(dc=1)
    for t in range(2):
        half = diag.at[:, :, :, lanes(core + 2 * t)]
        send(half, half, 4, partner)
    wait_bytes(diag.at[:, :, :, pl.ds(0, 256)], recv_sem.at[4])

    send(panel, wide.at[:, lanes(c)], 5, place(dc=2))
    send(panel, wide.at[:, lanes(c)], 6, partner)
    for peer in plane_only:
        to = place(**peer)
        send(part.at[lax.rem(to[0], NXY)], part_in.at[xy], 7, to)

    def assemble(i, carry):
        zi, q = i // NY, lax.rem(i, NY)
        even, odd = diag[zi, 2 * q], diag[zi, 2 * q + 1]
        first = pl.multiple_of(8 * i, 8)
        mat[pl.ds(first, 8), :] = jnp.concatenate([even[:4], odd[:4]], axis=0)
        mat[pl.ds(pl.multiple_of(256 + first, 8), 8), :] = jnp.concatenate(
            [even[4:], odd[4:]], axis=0
        )
        return carry

    lax.fori_loop(0, NZ * NY, assemble, 0)

    up, down = place(dz=1), place(dz=NZ - 1)

    def block(offset, step, way):
        ref = owned.at[lax.rem(z + offset, NZ)]
        if step == 3:
            ref = ref.at[pl.ds(4 * way, 4)]
        return ref

    def hop(step):
        for way, to in ((0, up), (1, down)):
            off = NZ - step if way == 0 else step
            ref = block(off, step, way)
            pltpu.make_async_remote_copy(
                src_ref=ref,
                dst_ref=ref,
                send_sem=ring_send.at[step, way],
                recv_sem=ring_recv.at[step, way],
                device_id=to,
                device_id_type=MESH,
            ).start()

    def landed(step):
        for way in range(2):
            off = NZ - step - 1 if way == 0 else step + 1
            wait_bytes(block(off, step, way), ring_recv.at[step, way])

    def between(k):
        if k == 0:
            wait_bytes(owned.at[0, pl.ds(0, 7)], recv_sem.at[3])
            hop(0)
        elif k == 1:
            landed(0)
            hop(1)
            wait_bytes(part.at[pl.ds(0, 7)], recv_sem.at[7])
            total = part[xy]
            for i in range(1, NXY):
                total = total + part_in[lax.rem(xy + i, NXY)]
            line[...] = total
            wait_bytes(wide.at[:, pl.ds(0, 128)], recv_sem.at[5])
            far = wide.at[:, lanes(place(dc=2)[1])]
            send(far, far, 8, partner)
        elif k == 2:
            landed(1)
            hop(2)
            for peer in line_peers:
                to = place(**peer)
                send(line.at[to[0] // NXY], line_in.at[z], 9, to)
        else:
            landed(2)
            hop(3)
            wait_bytes(line.at[pl.ds(0, 7)], recv_sem.at[9])
            total = line[z]
            for i in range(1, NZ):
                total = total + line_in[lax.rem(z + i, NZ)]
            proj[...] = total[:, :1024]
            head[c] = total[:, 1024:]

    def step(k, carry):
        eliminate(mat, k)
        for i in range(4):
            pl.when(k == i)(functools.partial(between, i))
        return carry

    lax.fori_loop(0, 4, step, 0)

    landed(3)
    for e in range(1, NC):
        send(head.at[c], head.at[c], 10, place(dc=e))

    inverse = halves(mat[...])

    def weigh(i, carry):
        rows = owned[pl.ds(2 * i, 2)].reshape(256, 512)
        weights[:, pl.ds(pl.multiple_of(i * 256, 256), 256)] = dot3(inverse, halves(rows), NT)
        return carry

    lax.fori_loop(0, 4, weigh, 0)
    wait_bytes(head.at[pl.ds(0, 3)], recv_sem.at[10])
    value = proj[...]
    for e in range(NC):
        value = value - exact(head[e], weights[pl.ds(128 * e, 128), :])
    proj[...] = value

    wait_bytes(wide.at[:, pl.ds(0, 128)], recv_sem.at[6])
    wait_bytes(wide.at[:, pl.ds(0, 128)], recv_sem.at[8])
    own_wide.wait()
    wait_bytes(panel.at[pl.ds(0, 56), :], send_sem.at[0])
    wait_bytes(panel.at[pl.ds(0, 48), :], send_sem.at[1])
    wait_bytes(diag.at[:, pl.ds(0, 5), :, pl.ds(0, 384)], send_sem.at[2])
    wait_bytes(owned.at[0, pl.ds(0, 7)], send_sem.at[3])
    wait_bytes(diag.at[:, :, :, pl.ds(0, 256)], send_sem.at[4])
    for i in (5, 6, 8):
        wait_bytes(wide.at[:, pl.ds(0, 128)], send_sem.at[i])
    wait_bytes(part.at[pl.ds(0, 7)], send_sem.at[7])
    wait_bytes(line.at[pl.ds(0, 7)], send_sem.at[9])
    wait_bytes(head.at[pl.ds(0, 3)], send_sem.at[10])
    for step_at in range(4):
        for way in range(2):
            wait_bytes(block(0, step_at, way), ring_send.at[step_at, way])


def exchange(cov_panel, cov_slab, frames):
    any_space = pl.BlockSpec(memory_space=pl.ANY)
    vmem = pl.BlockSpec(memory_space=pltpu.VMEM)
    return pl.pallas_call(
        exchange_kernel,
        out_shape=(
            jax.ShapeDtypeStruct((512, 1024), F32),
            jax.ShapeDtypeStruct((1024, 512), F32),
            jax.ShapeDtypeStruct((4, 1024), F32),
        ),
        in_specs=[any_space] * 3,
        out_specs=(vmem, any_space, vmem),
        scratch_shapes=[
            pltpu.VMEM((NZ, NXY, 8, 512), F32),
            pltpu.VMEM((512, 512), F32),
            pltpu.VMEM((NZ, NXY, 16, 512), F32),
            pltpu.VMEM((1024, 1024), F32),
            pltpu.VMEM((1024, 256), F32),
            pltpu.VMEM((1024, 128), F32),
            pltpu.VMEM((NXY, NZ, 4, 1152), F32),
            pltpu.VMEM((NXY, NZ, 4, 1152), F32),
            pltpu.VMEM((NZ, 4, 1152), F32),
            pltpu.VMEM((NZ, 4, 1152), F32),
            pltpu.VMEM((NC, 4, 128), F32),
            pltpu.SemaphoreType.DMA((5,)),
            pltpu.SemaphoreType.DMA((11,)),
            pltpu.SemaphoreType.DMA((11,)),
            pltpu.SemaphoreType.DMA((4, 2)),
            pltpu.SemaphoreType.DMA((4, 2)),
        ],
        compiler_params=pltpu.CompilerParams(
            collective_id=0, has_side_effects=True, vmem_limit_bytes=60 << 20
        ),
        name="exchange",
    )(cov_panel, cov_slab, frames)


def update_kernel(slab, wide, weights, out, high, low):
    @pl.when(pl.program_id(0) == 0)
    def _():
        high[...], low[...] = halves(weights[...])

    out[...] = slab[...] - dot3(halves(wide[...]), (high[...], low[...]), NN)


def update(cov_slab, wide, weights):
    rows = 256
    return pl.pallas_call(
        update_kernel,
        out_shape=jax.ShapeDtypeStruct((1024, 1024), F32),
        grid=(1024 // rows,),
        in_specs=[
            pl.BlockSpec((rows, 1024), lambda i: (i, 0)),
            pl.BlockSpec((rows, 512), lambda i: (i, 0)),
            pl.BlockSpec((512, 1024), lambda i: (0, 0), pipeline_mode=pl.Buffered(1)),
        ],
        out_specs=pl.BlockSpec((rows, 1024), lambda i: (i, 0)),
        scratch_shapes=[pltpu.VMEM((512, 1024), BF16), pltpu.VMEM((512, 1024), BF16)],
        compiler_params=pltpu.CompilerParams(vmem_limit_bytes=60 << 20),
        name="update",
    )(cov_slab, wide, weights)


def local(cov_panel, cov_slab, frames):
    weights, wide, projected = exchange(cov_panel, cov_slab, frames)
    return update(cov_slab, wide, weights), projected


def solution(mesh):
    placed = (P("rows", "cols"), P("rows", "cols"), P("rows", None))
    return jax.shard_map(
        local,
        mesh=mesh,
        in_specs=placed,
        out_specs=(P("rows", "cols"), P("rows", "cols")),
        check_vma=False,
    )
```

profile of v0, /device:TPU:1, one launch (start us, length us, event | category | flops | bytes accessed | tf_op | source)
XLA Modules:
  0.0 90.5 jit_solution(13859063436290428892)
XLA Ops:
  0.6 80.7 %exchange.1 = (f32[512,1024]{1,0:T(8,128)}, f32[1024,512]{1,0:T(8,128)}, f32[4,1024]{1,0:T(4,128)}) custom-call(f32[1024,128]{1,0:T(8,128)} %panel.1, f32[1024,1024]{1,0:T(8,128)} %slab.3, f32[1024,256]{1,0:T(8,128)} %frames.1), custom_call_target="tpu_custom_call" | custom-call | tf_op jit(solution)/shard_map/exchange/pallas_call | solution.py:362
  81.4 0.0 copy-start
  81.4 8.5 %update.1 = f32[1024,1024]{1,0:T(8,128)} custom-call(f32[1024,1024]{1,0:T(8,128)} %slab.3, f32[1024,512]{1,0:T(8,128)} %get-tuple-element.5.wide, f32[512,1024]{1,0:T(8,128)} %get-tuple-element.6.weights), custom_call_target="tpu_custom_call" | custom-call | tf_op jit(solution)/shard_map/update/pallas_call | solution.py:406
  89.9 0.0 copy-done
  89.9 0.6 copy.6
Async XLA Ops:
  81.4 8.5 %copy-start = (f32[4,1024]{1,0:T(4,128)S(1)}, f32[4,1024]{1,0:T(4,128)}, u32[]{:S(2)}) copy-start(f32[4,1024]{1,0:T(4,128)} %get-tuple-element.11) | copy-start | bytes 49156
where the time goes:
time: 90.7 us; the launch traced here: 90.5 us
  Pallas kernels  89.3 us (98%)
    pallas_call x1, Pallas kernels, exchange(): pl.pallas_call(exchange_kernel, out_shape=(jax.ShapeDtypeStruct((512, 102...  80.7 us
    pallas_call x1, Pallas kernels, update(): pl.pallas_call(update_kernel, out_shape=jax.ShapeDtypeStruct((1024, 1024)...  8.52 us

commit v1 on v0

--- a/solution.py
+++ b/solution.py
@@ -49,7 +49,7 @@
     return cols
 
 
-def block_inverse(parts):
+def block_inverse(parts, midway):
     lane = lax.broadcasted_iota(jnp.int32, (PIV, BLK), 1)
     row = lax.broadcasted_iota(jnp.int32, (PIV, BLK), 0)
     parts = list(parts)
@@ -62,6 +62,8 @@
         return (sums[0] + sums[1]) + (sums[2] + sums[3])
 
     for m in range(count):
+        if m == count // 2:
+            midway()
         cols = [
             [
                 jnp.broadcast_to(part[:, PIV * m + k : PIV * m + k + 1], (PIV, BLK))
@@ -85,14 +87,15 @@
     return jnp.concatenate(parts, axis=0)
 
 
-def eliminate(mat, k):
+def eliminate(mat, k, midway, inverted):
     size = mat.shape[0]
     at = pl.multiple_of(k * BLK, BLK)
     parts = [
         mat[pl.ds(pl.multiple_of(at + PIV * i, PIV), PIV), pl.ds(at, BLK)]
         for i in range(BLK // PIV)
     ]
-    inverse = block_inverse(parts)
+    inverse = block_inverse(parts, midway)
+    inverted()
     lane = lax.broadcasted_iota(jnp.int32, (BLK, size), 1) - at
     row = lax.broadcasted_iota(jnp.int32, (BLK, size), 0)
     inside = (lane >= 0) & (lane < BLK)
@@ -112,25 +115,31 @@
     panel,
     slab,
     frames,
-    weights,
+    high,
+    low,
+    rows_out,
     wide,
-    proj,
+    sums,
+    heads,
     diag,
+    first,
     mat,
     owned,
     slab_v,
     frames_v,
     panel_v,
     part,
-    part_in,
-    line,
-    line_in,
+    far_in,
+    near_in,
+    mid,
+    mid_in,
     head,
     load_sem,
     send_sem,
     recv_sem,
     ring_send,
     ring_recv,
+    store_sem,
 ):
     rows_at, c = lax.axis_index("rows"), lax.axis_index("cols")
     z, xy = rows_at // NXY, lax.rem(rows_at, NXY)
@@ -202,71 +211,98 @@
     own_wide.start()
     loads[1].wait()
     turned = halves(frames_v[...].T)
-    shared = dot3(turned, halves(panel_v[...]), NN)
-    for g in range(NZ * NXY):
-        part[g % NXY, g // NXY, :, 1024:1152] = shared[4 * g : 4 * g + 4, :]
+
+    def keep(value, at, width):
+        for g in range(NZ * NXY):
+            part[g % NY, g // NY % NX, g // NXY, :, pl.ds(at, width)] = value[4 * g : 4 * g + 4, :]
+
+    keep(dot3(turned, halves(panel_v[...]), NN), 1024, 128)
     loads[2].wait()
 
     def product(i, carry):
         at = pl.multiple_of(i * 256, 256)
-        value = dot3(turned, halves(slab_v[:, pl.ds(at, 256)]), NN)
-        for g in range(NZ * NXY):
-            part[g % NXY, g // NXY, :, pl.ds(at, 256)] = value[4 * g : 4 * g + 4, :]
+        keep(dot3(turned, halves(slab_v[:, pl.ds(at, 256)]), NN), at, 256)
         return carry
 
     lax.fori_loop(0, 4, product, 0)
 
     loads[3].wait()
     wait_bytes(diag.at[pl.ds(0, NZ - 1), xy, :, lanes(c)], recv_sem.at[0])
+
+    @pl.when(c == 0)
+    def _():
+        for peer in plane_peers:
+            send(
+                diag.at[pl.ds(0, NZ // 2), xy, :, pl.ds(0, 128)],
+                first.at[:, xy],
+                14,
+                place(**peer),
+            )
+        pltpu.make_async_copy(
+            diag.at[pl.ds(0, NZ // 2), xy, :, pl.ds(0, 128)], first.at[:, xy], load_sem.at[3]
+        ).start()
+
     same_core = [p for p in plane_peers if not p["dc"] & 1]
     for peer in same_core:
-        send(
-            diag.at[:, xy, :, lanes(c)], diag.at[:, xy, :, lanes(c)], 2, place(**peer)
-        )
+        send(diag.at[:, xy, :, lanes(c)], diag.at[:, xy, :, lanes(c)], 2, place(**peer))
     loads[4].wait()
     wait_bytes(owned.at[0, 0, :, pl.ds(0, 384)], recv_sem.at[1])
     plane_only = [p for p in plane_peers if not p["dc"]]
     for peer in plane_only:
         send(owned.at[z, xy], owned.at[z, xy], 3, place(**peer))
-
-    wait_bytes(diag.at[:, pl.ds(0, 5), :, pl.ds(0, 384)], recv_sem.at[2])
+    y_next, y_last = lax.rem(y + 1, NY), lax.rem(y + NY - 1, NY)
+    y_far = lax.rem(y + 2, NY)
+    send(part.at[y_far, 0], far_in.at[0], 7, place(dy=1))
+    send(part.at[y_far, 1], far_in.at[1], 9, place(dy=NY - 1))
+
     core = lax.rem(c, 2)
     partner = place(dc=1)
-    for t in range(2):
-        half = diag.at[:, :, :, lanes(core + 2 * t)]
-        send(half, half, 4, partner)
-    wait_bytes(diag.at[:, :, :, pl.ds(0, 256)], recv_sem.at[4])
-
-    send(panel, wide.at[:, lanes(c)], 5, place(dc=2))
-    send(panel, wide.at[:, lanes(c)], 6, partner)
-    for peer in plane_only:
-        to = place(**peer)
-        send(part.at[lax.rem(to[0], NXY)], part_in.at[xy], 7, to)
+
+    def interleave(source, i, width, upper):
+        zi, q = i // NY, lax.rem(i, NY)
+        even, odd = source[zi, 2 * q], source[zi, 2 * q + 1]
+        at = pl.multiple_of(8 * i, 8)
+        mat[pl.ds(at, 8), pl.ds(0, width)] = jnp.concatenate([even[:4], odd[:4]], axis=0)
+        if upper:
+            mat[pl.ds(pl.multiple_of(256 + at, 8), 8), :] = jnp.concatenate(
+                [even[4:], odd[4:]], axis=0
+            )
+
+    @pl.when(c == 0)
+    def _():
+        wait_bytes(first.at[:, pl.ds(0, NXY - 1)], recv_sem.at[14])
+        wait_bytes(first.at[:, 0], load_sem.at[3])
+
+    @pl.when(c != 0)
+    def _():
+        wait_bytes(first, recv_sem.at[14])
+
+    def assemble_first(i, carry):
+        interleave(first, i, 128, False)
+        return carry
 
     def assemble(i, carry):
-        zi, q = i // NY, lax.rem(i, NY)
-        even, odd = diag[zi, 2 * q], diag[zi, 2 * q + 1]
-        first = pl.multiple_of(8 * i, 8)
-        mat[pl.ds(first, 8), :] = jnp.concatenate([even[:4], odd[:4]], axis=0)
-        mat[pl.ds(pl.multiple_of(256 + first, 8), 8), :] = jnp.concatenate(
-            [even[4:], odd[4:]], axis=0
-        )
+        interleave(diag, i, 512, True)
         return carry
 
-    lax.fori_loop(0, NZ * NY, assemble, 0)
+    lax.fori_loop(0, NZ // 2 * NY, assemble_first, 0)
 
     up, down = place(dz=1), place(dz=NZ - 1)
 
-    def block(offset, step, way):
-        ref = owned.at[lax.rem(z + offset, NZ)]
+    def block(ref, offset, step, way):
+        ref = ref.at[lax.rem(z + offset, NZ)]
         if step == 3:
             ref = ref.at[pl.ds(4 * way, 4)]
         return ref
 
+    def store(step, way, off):
+        return pltpu.make_async_copy(
+            block(owned, off, step, way), block(rows_out, off, step, way), store_sem.at[step, way]
+        )
+
     def hop(step):
         for way, to in ((0, up), (1, down)):
-            off = NZ - step if way == 0 else step
-            ref = block(off, step, way)
+            ref = block(owned, NZ - step if way == 0 else step, step, way)
             pltpu.make_async_remote_copy(
                 src_ref=ref,
                 dst_ref=ref,
@@ -279,81 +315,111 @@
     def landed(step):
         for way in range(2):
             off = NZ - step - 1 if way == 0 else step + 1
-            wait_bytes(block(off, step, way), ring_recv.at[step, way])
-
-    def between(k):
+            wait_bytes(block(owned, off, step, way), ring_recv.at[step, way])
+            store(step, way, off).start()
+
+    own_rows = pltpu.make_async_copy(owned.at[z], rows_out.at[z], load_sem.at[4])
+    own_head = pltpu.make_async_copy(head, heads.at[c], load_sem.at[1])
+    fifteen = part.at[pl.ds(0, 3), 0, pl.ds(0, 5)]
+    others = [(a, d) for a in range(NX) for d in range(NZ) if a or d]
+
+    def midway(k):
         if k == 0:
+            wait_bytes(diag.at[:, pl.ds(0, 5), :, pl.ds(0, 384)], recv_sem.at[2])
+            for t in range(2):
+                half = diag.at[:, :, :, lanes(core + 2 * t)]
+                send(half, half, 4, partner)
+            wait_bytes(far_in.at[0], recv_sem.at[7])
+            wait_bytes(far_in.at[1], recv_sem.at[9])
+            part[y_next, 0] = part[y_next, 0] + far_in[0]
+            part[y_last, 1] = part[y_last, 1] + far_in[1]
             wait_bytes(owned.at[0, pl.ds(0, 7)], recv_sem.at[3])
             hop(0)
+            own_rows.start()
+            send(part.at[y_next], near_in.at[0], 11, place(dy=1))
+            send(part.at[y_last], near_in.at[1], 12, place(dy=NY - 1))
+            send(panel, wide.at[:, lanes(c)], 5, place(dc=2))
         elif k == 1:
             landed(0)
             hop(1)
-            wait_bytes(part.at[pl.ds(0, 7)], recv_sem.at[7])
-            total = part[xy]
-            for i in range(1, NXY):
-                total = total + part_in[lax.rem(xy + i, NXY)]
-            line[...] = total
+            send(panel, wide.at[:, lanes(c)], 6, partner)
+            wait_bytes(near_in.at[0], recv_sem.at[11])
+            wait_bytes(near_in.at[1], recv_sem.at[12])
+            mid[...] = part[y] + (near_in[0] + near_in[1])
+        elif k == 2:
+            landed(1)
+            hop(2)
             wait_bytes(wide.at[:, pl.ds(0, 128)], recv_sem.at[5])
             far = wide.at[:, lanes(place(dc=2)[1])]
             send(far, far, 8, partner)
-        elif k == 2:
-            landed(1)
-            hop(2)
-            for peer in line_peers:
-                to = place(**peer)
-                send(line.at[to[0] // NXY], line_in.at[z], 9, to)
         else:
             landed(2)
             hop(3)
-            wait_bytes(line.at[pl.ds(0, 7)], recv_sem.at[9])
-            total = line[z]
-            for i in range(1, NZ):
-                total = total + line_in[lax.rem(z + i, NZ)]
-            proj[...] = total[:, :1024]
-            head[c] = total[:, 1024:]
+            for e in range(1, NC):
+                send(head, heads.at[c], 10, place(dc=e))
+            own_head.start()
+
+    def inverted(k):
+        if k == 0:
+            wait_bytes(diag.at[:, :, :, pl.ds(0, 256)], recv_sem.at[4])
+            lax.fori_loop(0, NZ * NY, assemble, 0)
+        elif k == 1:
+            for dx, dz in others:
+                to = place(dx=dx, dz=dz)
+                zt, xt = to[0] // NXY, lax.rem(to[0], NXY) // NY
+                send(mid.at[xt, zt], mid_in.at[x, z], 13, to)
+        elif k == 2:
+            wait_bytes(fifteen, recv_sem.at[13])
+            total = mid[x, z]
+            for dx, dz in others:
+                total = total + mid_in[lax.rem(x + dx, NX), lax.rem(z + dz, NZ)]
+            sums[...] = total[:, :1024]
+            head[...] = total[:, 1024:]
+
+    def at_each(k, action, count):
+        for i in range(count):
+            pl.when(k == i)(functools.partial(action, i))
 
     def step(k, carry):
-        eliminate(mat, k)
-        for i in range(4):
-            pl.when(k == i)(functools.partial(between, i))
+        eliminate(
+            mat, k, lambda: at_each(k, midway, 4), lambda: at_each(k, inverted, 3)
+        )
         return carry
 
     lax.fori_loop(0, 4, step, 0)
 
+    high[...], low[...] = halves(mat[...])
     landed(3)
-    for e in range(1, NC):
-        send(head.at[c], head.at[c], 10, place(dc=e))
-
-    inverse = halves(mat[...])
-
-    def weigh(i, carry):
-        rows = owned[pl.ds(2 * i, 2)].reshape(256, 512)
-        weights[:, pl.ds(pl.multiple_of(i * 256, 256), 256)] = dot3(inverse, halves(rows), NT)
-        return carry
-
-    lax.fori_loop(0, 4, weigh, 0)
-    wait_bytes(head.at[pl.ds(0, 3)], recv_sem.at[10])
-    value = proj[...]
-    for e in range(NC):
-        value = value - exact(head[e], weights[pl.ds(128 * e, 128), :])
-    proj[...] = value
+    wait_bytes(heads.at[pl.ds(0, 3)], recv_sem.at[10])
 
     wait_bytes(wide.at[:, pl.ds(0, 128)], recv_sem.at[6])
     wait_bytes(wide.at[:, pl.ds(0, 128)], recv_sem.at[8])
     own_wide.wait()
+    own_rows.wait()
+    own_head.wait()
     wait_bytes(panel.at[pl.ds(0, 56), :], send_sem.at[0])
     wait_bytes(panel.at[pl.ds(0, 48), :], send_sem.at[1])
     wait_bytes(diag.at[:, pl.ds(0, 5), :, pl.ds(0, 384)], send_sem.at[2])
     wait_bytes(owned.at[0, pl.ds(0, 7)], send_sem.at[3])
+
+    @pl.when(c == 0)
+    def _():
+        for _ in plane_peers:
+            wait_bytes(first.at[:, 0], send_sem.at[14])
+
     wait_bytes(diag.at[:, :, :, pl.ds(0, 256)], send_sem.at[4])
     for i in (5, 6, 8):
         wait_bytes(wide.at[:, pl.ds(0, 128)], send_sem.at[i])
-    wait_bytes(part.at[pl.ds(0, 7)], send_sem.at[7])
-    wait_bytes(line.at[pl.ds(0, 7)], send_sem.at[9])
-    wait_bytes(head.at[pl.ds(0, 3)], send_sem.at[10])
+    for i in (7, 9):
+        wait_bytes(far_in.at[0], send_sem.at[i])
+    for i in (11, 12):
+        wait_bytes(near_in.at[0], send_sem.at[i])
+    wait_bytes(heads.at[pl.ds(0, 3)], send_sem.at[10])
+    wait_bytes(fifteen, send_sem.at[13])
     for step_at in range(4):
         for way in range(2):
-            wait_bytes(block(0, step_at, way), ring_send.at[step_at, way])
+            wait_bytes(block(owned, 0, step_at, way), ring_send.at[step_at, way])
+            store(step_at, way, 0).wait()
 
 
 def exchange(cov_panel, cov_slab, frames):
@@ -362,27 +428,33 @@
     return pl.pallas_call(
         exchange_kernel,
         out_shape=(
-            jax.ShapeDtypeStruct((512, 1024), F32),
+            jax.ShapeDtypeStruct((512, 512), BF16),
+            jax.ShapeDtypeStruct((512, 512), BF16),
+            jax.ShapeDtypeStruct((NZ, NXY, 16, 512), F32),
             jax.ShapeDtypeStruct((1024, 512), F32),
             jax.ShapeDtypeStruct((4, 1024), F32),
+            jax.ShapeDtypeStruct((NC, 4, 128), F32),
         ),
         in_specs=[any_space] * 3,
-        out_specs=(vmem, any_space, vmem),
+        out_specs=(vmem, vmem, any_space, any_space, vmem, any_space),
         scratch_shapes=[
             pltpu.VMEM((NZ, NXY, 8, 512), F32),
+            pltpu.VMEM((NZ // 2, NXY, 8, 128), F32),
             pltpu.VMEM((512, 512), F32),
             pltpu.VMEM((NZ, NXY, 16, 512), F32),
             pltpu.VMEM((1024, 1024), F32),
             pltpu.VMEM((1024, 256), F32),
             pltpu.VMEM((1024, 128), F32),
-            pltpu.VMEM((NXY, NZ, 4, 1152), F32),
-            pltpu.VMEM((NXY, NZ, 4, 1152), F32),
-            pltpu.VMEM((NZ, 4, 1152), F32),
-            pltpu.VMEM((NZ, 4, 1152), F32),
-            pltpu.VMEM((NC, 4, 128), F32),
+            pltpu.VMEM((NY, NX, NZ, 4, 1152), F32),
+            pltpu.VMEM((2, NZ, 4, 1152), F32),
+            pltpu.VMEM((2, NX, NZ, 4, 1152), F32),
+            pltpu.VMEM((NX, NZ, 4, 1152), F32),
+            pltpu.VMEM((NX, NZ, 4, 1152), F32),
+            pltpu.VMEM((4, 128), F32),
             pltpu.SemaphoreType.DMA((5,)),
-            pltpu.SemaphoreType.DMA((11,)),
-            pltpu.SemaphoreType.DMA((11,)),
+            pltpu.SemaphoreType.DMA((15,)),
+            pltpu.SemaphoreType.DMA((15,)),
+            pltpu.SemaphoreType.DMA((4, 2)),
             pltpu.SemaphoreType.DMA((4, 2)),
             pltpu.SemaphoreType.DMA((4, 2)),
         ],
@@ -393,35 +465,53 @@
     )(cov_panel, cov_slab, frames)
 
 
-def update_kernel(slab, wide, weights, out, high, low):
+COLS = 512
+
+
+def update_kernel(high, low, rows, wide, slab, sums, heads, out, proj, wide_h, wide_l):
     @pl.when(pl.program_id(0) == 0)
     def _():
-        high[...], low[...] = halves(weights[...])
-
-    out[...] = slab[...] - dot3(halves(wide[...]), (high[...], low[...]), NN)
-
-
-def update(cov_slab, wide, weights):
-    rows = 256
+        wide_h[...], wide_l[...] = halves(wide[...])
+
+    weights = dot3((high[...], low[...]), halves(rows[...].reshape(COLS, 512)), NT)
+    value = sums[...]
+    for e in range(NC):
+        value = value - exact(heads[e], weights[128 * e : 128 * e + 128, :])
+    proj[...] = value
+    out[...] = slab[...] - dot3((wide_h[...], wide_l[...]), halves(weights), NN)
+
+
+def update(high, low, rows, wide, cov_slab, sums, heads):
+    once = pl.Buffered(1)
     return pl.pallas_call(
         update_kernel,
-        out_shape=jax.ShapeDtypeStruct((1024, 1024), F32),
-        grid=(1024 // rows,),
+        out_shape=(
+            jax.ShapeDtypeStruct((1024, 1024), F32),
+            jax.ShapeDtypeStruct((4, 1024), F32),
+        ),
+        grid=(1024 // COLS,),
         in_specs=[
-            pl.BlockSpec((rows, 1024), lambda i: (i, 0)),
-            pl.BlockSpec((rows, 512), lambda i: (i, 0)),
-            pl.BlockSpec((512, 1024), lambda i: (0, 0), pipeline_mode=pl.Buffered(1)),
+            pl.BlockSpec((512, 512), lambda i: (0, 0), pipeline_mode=once),
+            pl.BlockSpec((512, 512), lambda i: (0, 0), pipeline_mode=once),
+            pl.BlockSpec((COLS // 128, NXY, 16, 512), lambda i: (i, 0, 0, 0)),
+            pl.BlockSpec((1024, 512), lambda i: (0, 0), pipeline_mode=once),
+            pl.BlockSpec((1024, COLS), lambda i: (0, i)),
+            pl.BlockSpec((4, COLS), lambda i: (0, i)),
+            pl.BlockSpec((NC, 4, 128), lambda i: (0, 0, 0), pipeline_mode=once),
         ],
-        out_specs=pl.BlockSpec((rows, 1024), lambda i: (i, 0)),
-        scratch_shapes=[pltpu.VMEM((512, 1024), BF16), pltpu.VMEM((512, 1024), BF16)],
+        out_specs=(
+            pl.BlockSpec((1024, COLS), lambda i: (0, i)),
+            pl.BlockSpec((4, COLS), lambda i: (0, i)),
+        ),
+        scratch_shapes=[pltpu.VMEM((1024, 512), BF16), pltpu.VMEM((1024, 512), BF16)],
         compiler_params=pltpu.CompilerParams(vmem_limit_bytes=60 << 20),
         name="update",
-    )(cov_slab, wide, weights)
+    )(high, low, rows, wide, cov_slab, sums, heads)
 
 
 def local(cov_panel, cov_slab, frames):
-    weights, wide, projected = exchange(cov_panel, cov_slab, frames)
-    return update(cov_slab, wide, weights), projected
+    high, low, rows, wide, sums, heads = exchange(cov_panel, cov_slab, frames)
+    return update(high, low, rows, wide, cov_slab, sums, heads)
 
 
 def solution(mesh):

time: 90.7 us -> 80.2 us (0.88)
  Pallas kernels: 89.3 us -> 79 us
    pallas_call x2, Pallas kernels: 89.3 us -> 79 us  [the longest x1 67.3 us: exchange(): pl.pallas_call(exchange_kernel, out_shape=(jax.ShapeDtypeStruct((512, 512...]
where the time goes in v1:
time: 80.2 us; the launch traced here: 79.6 us
  Pallas kernels  79 us (99%)
    pallas_call x1, Pallas kernels, exchange(): pl.pallas_call(exchange_kernel, out_shape=(jax.ShapeDtypeStruct((512, 512...  67.3 us
    pallas_call x1, Pallas kernels, update(): pl.pallas_call(update_kernel, out_shape=(jax.ShapeDtypeStruct((1024, 1024...  11.7 us

profile of v1, /device:TPU:1, one launch (start us, length us, event | category | flops | bytes accessed | tf_op | source)
XLA Modules:
  0.0 79.6 jit_solution(12699371699522603695)
XLA Ops:
  0.6 67.3 %exchange.1 = (bf16[512,512]{1,0:T(8,128)(2,1)}, bf16[512,512]{1,0:T(8,128)(2,1)}, f32[8,8,16,512]{3,2,1,0:T(8,128)}, f32[1024,512]{1,0:T(8,128)}, f32[4,1024]{1,0:T(4,128)}, /*index=5*/f32[4,4,128]{2,1,0:T(4,128)}) custom-call(f32[1024,128]{1,0:T(8,128)} %panel.1, f32[1024,1024]{1,0:T(8,128)} %slab.3, f32[1024,256]{1,0:T(8,128)} %frames.1), custom_call_target="tpu_custom_call" | custom-call | tf_op jit(solution)/shard_map/exchange/pallas_call | solution.py:428
  67.9 11.7 %update.1 = (f32[1024,1024]{1,0:T(8,128)}, f32[4,1024]{1,0:T(4,128)}) custom-call(bf16[512,512]{1,0:T(8,128)(2,1)} %get-tuple-element.8.high, bf16[512,512]{1,0:T(8,128)(2,1)} %get-tuple-element.9.low, f32[8,8,16,512]{3,2,1,0:T(8,128)} %get-tuple-element.10.rows, f32[1024,512]{1,0:T(8,128)} %get-tuple-element.11.wide, f32[1024,1024]{1,0:T(8,128)} %slab.3, ...), custom_call_target="tpu_custom_call" | custom-call | tf_op jit(solution)/shard_map/update/pallas_call | solution.py:486

commit v2 on v1

--- a/solution.py
+++ b/solution.py
@@ -34,67 +34,73 @@
     return dot(lh, rh) + (dot(lh, rl) + dot(ll, rh))
 
 
+def down(rows, k):
+    return jnp.broadcast_to(rows[k : k + 1, :], (PIV, 128))
+
+
+def across(rows, k):
+    return jnp.broadcast_to(rows[:, k : k + 1], (PIV, 128))
+
+
+def total(terms):
+    sums = terms[:4]
+    for i, term in enumerate(terms[4:]):
+        sums[i % 4] = sums[i % 4] + term
+    return (sums[0] + sums[1]) + (sums[2] + sums[3])
+
+
 def small_inverse(cols):
     row = lax.broadcasted_iota(jnp.int32, (PIV, 128), 0)
     cols = list(cols)
-    for j in range(PIV):
-        across = [jnp.broadcast_to(col[j : j + 1, :], (PIV, 128)) for col in cols]
-        recip = 1.0 / across[j]
-        here = row == j
-        pivot = jnp.where(here, -1.0, cols[j])
+    for j in range(0, PIV, 2):
+        upper = [down(col, j) for col in cols]
+        lower = [down(col, j + 1) for col in cols]
+        a, b, d = upper[j], upper[j + 1], lower[j + 1]
+        recip = 1.0 / (a * d - b * b)
+        inv_a, inv_b, inv_d = d * recip, -(b * recip), a * recip
+        first, second = row == j, row == j + 1
+        here = first | second
+        left = jnp.where(first, -1.0, jnp.where(second, 0.0, cols[j]))
+        right = jnp.where(second, -1.0, jnp.where(first, 0.0, cols[j + 1]))
+        left, right = left * inv_a + right * inv_b, left * inv_b + right * inv_d
         for k in range(PIV):
-            if k != j:
-                cols[k] = jnp.where(here, 0.0, cols[k]) - pivot * (across[k] * recip)
-        cols[j] = -pivot * recip
+            if k not in (j, j + 1):
+                cols[k] = jnp.where(here, 0.0, cols[k]) - (left * upper[k] + right * lower[k])
+        cols[j], cols[j + 1] = -left, -right
     return cols
 
 
-def block_inverse(parts, midway):
+def block_inverse(block, midway):
     lane = lax.broadcasted_iota(jnp.int32, (PIV, BLK), 1)
     row = lax.broadcasted_iota(jnp.int32, (PIV, BLK), 0)
-    parts = list(parts)
+    lanes = lax.broadcasted_iota(jnp.int32, (BLK, BLK), 1)
     count = BLK // PIV
-
-    def total(terms):
-        sums = terms[:4]
-        for i, term in enumerate(terms[4:]):
-            sums[i % 4] = sums[i % 4] + term
-        return (sums[0] + sums[1]) + (sums[2] + sums[3])
-
+    rows = block[0:PIV, :]
     for m in range(count):
         if m == count // 2:
             midway()
-        cols = [
-            [
-                jnp.broadcast_to(part[:, PIV * m + k : PIV * m + k + 1], (PIV, BLK))
-                for k in range(PIV)
-            ]
-            for part in parts
-        ]
-        inverse = small_inverse(cols[m])
-        inside = (lane >= PIV * m) & (lane < PIV * m + PIV)
-        panel = jnp.where(inside, jnp.where(lane - PIV * m == row, 1.0, 0.0), parts[m])
-        solved = total(
-            [inverse[k] * jnp.broadcast_to(panel[k : k + 1, :], (PIV, BLK)) for k in range(PIV)]
-        )
-        spread = [jnp.broadcast_to(solved[k : k + 1, :], (PIV, BLK)) for k in range(PIV)]
-        for t in range(1, count):
-            i = (m + t) % count
-            parts[i] = jnp.where(inside, 0.0, parts[i]) - total(
-                [cols[i][k] * spread[k] for k in range(PIV)]
+        at = PIV * m
+        inverse = small_inverse([across(rows, at + k) for k in range(PIV)])
+        inside = (lane >= at) & (lane < at + PIV)
+        panel = jnp.where(inside, jnp.where(lane - at == row, 1.0, 0.0), rows)
+        solved = total([inverse[k] * down(panel, k) for k in range(PIV)])
+        if m < count - 1:
+            ahead = block[at + PIV : at + 2 * PIV, :]
+            rows = jnp.where(inside, 0.0, ahead) - total(
+                [across(ahead, at + k) * down(solved, k) for k in range(PIV)]
             )
-        parts[m] = solved
-    return jnp.concatenate(parts, axis=0)
-
-
-def eliminate(mat, k, midway, inverted):
+        whole = block[...]
+        cleared = jnp.where((lanes >= at) & (lanes < at + PIV), 0.0, whole)
+        block[...] = cleared - exact(whole[:, at : at + PIV], solved)
+        block[at : at + PIV, :] = solved
+    return block[...]
+
+
+def eliminate(mat, block, k, midway, inverted):
     size = mat.shape[0]
     at = pl.multiple_of(k * BLK, BLK)
-    parts = [
-        mat[pl.ds(pl.multiple_of(at + PIV * i, PIV), PIV), pl.ds(at, BLK)]
-        for i in range(BLK // PIV)
-    ]
-    inverse = block_inverse(parts, midway)
+    block[...] = mat[pl.ds(at, BLK), pl.ds(at, BLK)]
+    inverse = block_inverse(block, midway)
     inverted()
     lane = lax.broadcasted_iota(jnp.int32, (BLK, size), 1) - at
     row = lax.broadcasted_iota(jnp.int32, (BLK, size), 0)
@@ -124,6 +130,7 @@
     diag,
     first,
     mat,
+    pivots,
     owned,
     slab_v,
     frames_v,
@@ -287,7 +294,7 @@
 
     lax.fori_loop(0, NZ // 2 * NY, assemble_first, 0)
 
-    up, down = place(dz=1), place(dz=NZ - 1)
+    above, below = place(dz=1), place(dz=NZ - 1)
 
     def block(ref, offset, step, way):
         ref = ref.at[lax.rem(z + offset, NZ)]
@@ -301,7 +308,7 @@
         )
 
     def hop(step):
-        for way, to in ((0, up), (1, down)):
+        for way, to in ((0, above), (1, below)):
             ref = block(owned, NZ - step if way == 0 else step, step, way)
             pltpu.make_async_remote_copy(
                 src_ref=ref,
@@ -382,7 +389,11 @@
 
     def step(k, carry):
         eliminate(
-            mat, k, lambda: at_each(k, midway, 4), lambda: at_each(k, inverted, 3)
+            mat,
+            pivots,
+            k,
+            lambda: at_each(k, midway, 4),
+            lambda: at_each(k, inverted, 3),
         )
         return carry
 
@@ -441,6 +452,7 @@
             pltpu.VMEM((NZ, NXY, 8, 512), F32),
             pltpu.VMEM((NZ // 2, NXY, 8, 128), F32),
             pltpu.VMEM((512, 512), F32),
+            pltpu.VMEM((BLK, BLK), F32),
             pltpu.VMEM((NZ, NXY, 16, 512), F32),
             pltpu.VMEM((1024, 1024), F32),
             pltpu.VMEM((1024, 256), F32),

time: 80.2 us -> 74.7 us (0.931)
  Pallas kernels: 79 us -> 73.6 us
    pallas_call x1, Pallas kernels: 67.3 us -> 61.9 us  [exchange(): pl.pallas_call(exchange_kernel, out_shape=(jax.ShapeDtypeStruct((512, 512...]
where the time goes in v2:
time: 74.7 us; the launch traced here: 74.2 us
  Pallas kernels  73.6 us (99%)
    pallas_call x1, Pallas kernels, exchange(): pl.pallas_call(exchange_kernel, out_shape=(jax.ShapeDtypeStruct((512, 512...  61.9 us
    pallas_call x1, Pallas kernels, update(): pl.pallas_call(update_kernel, out_shape=(jax.ShapeDtypeStruct((1024, 1024...  11.7 us

profile of v2, /device:TPU:1, one launch (start us, length us, event | category | flops | bytes accessed | tf_op | source)
XLA Modules:
  0.0 74.2 jit_solution(7089189457754827945)
XLA Ops:
  0.6 61.9 %exchange.1 = (bf16[512,512]{1,0:T(8,128)(2,1)}, bf16[512,512]{1,0:T(8,128)(2,1)}, f32[8,8,16,512]{3,2,1,0:T(8,128)}, f32[1024,512]{1,0:T(8,128)}, f32[4,1024]{1,0:T(4,128)}, /*index=5*/f32[4,4,128]{2,1,0:T(4,128)}) custom-call(f32[1024,128]{1,0:T(8,128)} %panel.1, f32[1024,1024]{1,0:T(8,128)} %slab.3, f32[1024,256]{1,0:T(8,128)} %frames.1), custom_call_target="tpu_custom_call" | custom-call | tf_op jit(solution)/shard_map/exchange/pallas_call | solution.py:439
  62.5 11.7 %update.1 = (f32[1024,1024]{1,0:T(8,128)}, f32[4,1024]{1,0:T(4,128)}) custom-call(bf16[512,512]{1,0:T(8,128)(2,1)} %get-tuple-element.8.high, bf16[512,512]{1,0:T(8,128)(2,1)} %get-tuple-element.9.low, f32[8,8,16,512]{3,2,1,0:T(8,128)} %get-tuple-element.10.rows, f32[1024,512]{1,0:T(8,128)} %get-tuple-element.11.wide, f32[1024,1024]{1,0:T(8,128)} %slab.3, ...), custom_call_target="tpu_custom_call" | custom-call | tf_op jit(solution)/shard_map/update/pallas_call | solution.py:498

commit v3 on v2

--- a/solution.py
+++ b/solution.py
@@ -234,6 +234,13 @@
     lax.fori_loop(0, 4, product, 0)
 
     loads[3].wait()
+    loads[4].wait()
+    wait_bytes(owned.at[0, 0, :, pl.ds(0, 384)], recv_sem.at[1])
+    y_next, y_last = lax.rem(y + 1, NY), lax.rem(y + NY - 1, NY)
+    y_far = lax.rem(y + 2, NY)
+    send(part.at[y_far, 0], far_in.at[0], 7, place(dy=1))
+    send(part.at[y_far, 1], far_in.at[1], 9, place(dy=NY - 1))
+
     wait_bytes(diag.at[pl.ds(0, NZ - 1), xy, :, lanes(c)], recv_sem.at[0])
 
     @pl.when(c == 0)
@@ -249,19 +256,12 @@
             diag.at[pl.ds(0, NZ // 2), xy, :, pl.ds(0, 128)], first.at[:, xy], load_sem.at[3]
         ).start()
 
+    plane_only = [p for p in plane_peers if not p["dc"]]
+    for peer in plane_only:
+        send(owned.at[z, xy], owned.at[z, xy], 3, place(**peer))
     same_core = [p for p in plane_peers if not p["dc"] & 1]
     for peer in same_core:
         send(diag.at[:, xy, :, lanes(c)], diag.at[:, xy, :, lanes(c)], 2, place(**peer))
-    loads[4].wait()
-    wait_bytes(owned.at[0, 0, :, pl.ds(0, 384)], recv_sem.at[1])
-    plane_only = [p for p in plane_peers if not p["dc"]]
-    for peer in plane_only:
-        send(owned.at[z, xy], owned.at[z, xy], 3, place(**peer))
-    y_next, y_last = lax.rem(y + 1, NY), lax.rem(y + NY - 1, NY)
-    y_far = lax.rem(y + 2, NY)
-    send(part.at[y_far, 0], far_in.at[0], 7, place(dy=1))
-    send(part.at[y_far, 1], far_in.at[1], 9, place(dy=NY - 1))
-
     core = lax.rem(c, 2)
     partner = place(dc=1)
 
@@ -275,6 +275,50 @@
                 [even[4:], odd[4:]], axis=0
             )
 
+    above, below = place(dz=1), place(dz=NZ - 1)
+
+    def half(ref, offset, part_at):
+        return ref.at[lax.rem(z + offset, NZ), pl.ds(4 * part_at, 4)]
+
+    def ways(step, part_at):
+        return ((0, above), (1, below)) if step < 3 else ((part_at, (above, below)[part_at]),)
+
+    def store(step, way, part_at, off):
+        return pltpu.make_async_copy(
+            half(owned, off, part_at), half(rows_out, off, part_at), store_sem.at[step, way, part_at]
+        )
+
+    def hop(step, part_at):
+        for way, to in ways(step, part_at):
+            ref = half(owned, NZ - step if way == 0 else step, part_at)
+            pltpu.make_async_remote_copy(
+                src_ref=ref,
+                dst_ref=ref,
+                send_sem=ring_send.at[step, way, part_at],
+                recv_sem=ring_recv.at[step, way, part_at],
+                device_id=to,
+                device_id_type=MESH,
+            ).start()
+
+    def landed(step, part_at):
+        for way, _ in ways(step, part_at):
+            off = NZ - step - 1 if way == 0 else step + 1
+            wait_bytes(half(owned, off, part_at), ring_recv.at[step, way, part_at])
+            store(step, way, part_at, off).start()
+
+    def onward(step, part_at):
+        landed(step, part_at)
+        hop(step + 1, part_at)
+
+    own_rows = pltpu.make_async_copy(owned.at[z], rows_out.at[z], load_sem.at[4])
+    own_head = pltpu.make_async_copy(head, heads.at[c], load_sem.at[1])
+    fifteen = part.at[pl.ds(0, 3), 0, pl.ds(0, 5)]
+    others = [(a, d) for a in range(NX) for d in range(NZ) if a or d]
+
+    wait_bytes(far_in.at[0], recv_sem.at[7])
+    wait_bytes(far_in.at[1], recv_sem.at[9])
+    part[y_next, 0] = part[y_next, 0] + far_in[0]
+    part[y_last, 1] = part[y_last, 1] + far_in[1]
     @pl.when(c == 0)
     def _():
         wait_bytes(first.at[:, pl.ds(0, NXY - 1)], recv_sem.at[14])
@@ -284,6 +328,11 @@
     def _():
         wait_bytes(first, recv_sem.at[14])
 
+    wait_bytes(owned.at[0, pl.ds(0, 7)], recv_sem.at[3])
+    hop(0, 0)
+    hop(0, 1)
+    own_rows.start()
+
     def assemble_first(i, carry):
         interleave(first, i, 128, False)
         return carry
@@ -293,75 +342,33 @@
         return carry
 
     lax.fori_loop(0, NZ // 2 * NY, assemble_first, 0)
-
-    above, below = place(dz=1), place(dz=NZ - 1)
-
-    def block(ref, offset, step, way):
-        ref = ref.at[lax.rem(z + offset, NZ)]
-        if step == 3:
-            ref = ref.at[pl.ds(4 * way, 4)]
-        return ref
-
-    def store(step, way, off):
-        return pltpu.make_async_copy(
-            block(owned, off, step, way), block(rows_out, off, step, way), store_sem.at[step, way]
-        )
-
-    def hop(step):
-        for way, to in ((0, above), (1, below)):
-            ref = block(owned, NZ - step if way == 0 else step, step, way)
-            pltpu.make_async_remote_copy(
-                src_ref=ref,
-                dst_ref=ref,
-                send_sem=ring_send.at[step, way],
-                recv_sem=ring_recv.at[step, way],
-                device_id=to,
-                device_id_type=MESH,
-            ).start()
-
-    def landed(step):
-        for way in range(2):
-            off = NZ - step - 1 if way == 0 else step + 1
-            wait_bytes(block(owned, off, step, way), ring_recv.at[step, way])
-            store(step, way, off).start()
-
-    own_rows = pltpu.make_async_copy(owned.at[z], rows_out.at[z], load_sem.at[4])
-    own_head = pltpu.make_async_copy(head, heads.at[c], load_sem.at[1])
-    fifteen = part.at[pl.ds(0, 3), 0, pl.ds(0, 5)]
-    others = [(a, d) for a in range(NX) for d in range(NZ) if a or d]
+    send(part.at[y_next], near_in.at[0], 11, place(dy=1))
+    send(part.at[y_last], near_in.at[1], 12, place(dy=NY - 1))
 
     def midway(k):
         if k == 0:
             wait_bytes(diag.at[:, pl.ds(0, 5), :, pl.ds(0, 384)], recv_sem.at[2])
             for t in range(2):
-                half = diag.at[:, :, :, lanes(core + 2 * t)]
-                send(half, half, 4, partner)
-            wait_bytes(far_in.at[0], recv_sem.at[7])
-            wait_bytes(far_in.at[1], recv_sem.at[9])
-            part[y_next, 0] = part[y_next, 0] + far_in[0]
-            part[y_last, 1] = part[y_last, 1] + far_in[1]
-            wait_bytes(owned.at[0, pl.ds(0, 7)], recv_sem.at[3])
-            hop(0)
-            own_rows.start()
-            send(part.at[y_next], near_in.at[0], 11, place(dy=1))
-            send(part.at[y_last], near_in.at[1], 12, place(dy=NY - 1))
+                other = diag.at[:, :, :, lanes(core + 2 * t)]
+                send(other, other, 4, partner)
             send(panel, wide.at[:, lanes(c)], 5, place(dc=2))
         elif k == 1:
-            landed(0)
-            hop(1)
-            send(panel, wide.at[:, lanes(c)], 6, partner)
             wait_bytes(near_in.at[0], recv_sem.at[11])
             wait_bytes(near_in.at[1], recv_sem.at[12])
             mid[...] = part[y] + (near_in[0] + near_in[1])
+            onward(0, 1)
+            for dx, dz in others:
+                to = place(dx=dx, dz=dz)
+                zt, xt = to[0] // NXY, lax.rem(to[0], NXY) // NY
+                send(mid.at[xt, zt], mid_in.at[x, z], 13, to)
+            send(panel, wide.at[:, lanes(c)], 6, partner)
         elif k == 2:
-            landed(1)
-            hop(2)
+            onward(1, 1)
             wait_bytes(wide.at[:, pl.ds(0, 128)], recv_sem.at[5])
             far = wide.at[:, lanes(place(dc=2)[1])]
             send(far, far, 8, partner)
         else:
-            landed(2)
-            hop(3)
+            onward(2, 1)
             for e in range(1, NC):
                 send(head, heads.at[c], 10, place(dc=e))
             own_head.start()
@@ -370,12 +377,11 @@
         if k == 0:
             wait_bytes(diag.at[:, :, :, pl.ds(0, 256)], recv_sem.at[4])
             lax.fori_loop(0, NZ * NY, assemble, 0)
+            onward(0, 0)
         elif k == 1:
-            for dx, dz in others:
-                to = place(dx=dx, dz=dz)
-                zt, xt = to[0] // NXY, lax.rem(to[0], NXY) // NY
-                send(mid.at[xt, zt], mid_in.at[x, z], 13, to)
+            onward(1, 0)
         elif k == 2:
+            onward(2, 0)
             wait_bytes(fifteen, recv_sem.at[13])
             total = mid[x, z]
             for dx, dz in others:
@@ -400,7 +406,8 @@
     lax.fori_loop(0, 4, step, 0)
 
     high[...], low[...] = halves(mat[...])
-    landed(3)
+    landed(3, 0)
+    landed(3, 1)
     wait_bytes(heads.at[pl.ds(0, 3)], recv_sem.at[10])
 
     wait_bytes(wide.at[:, pl.ds(0, 128)], recv_sem.at[6])
@@ -428,9 +435,10 @@
     wait_bytes(heads.at[pl.ds(0, 3)], send_sem.at[10])
     wait_bytes(fifteen, send_sem.at[13])
     for step_at in range(4):
-        for way in range(2):
-            wait_bytes(block(owned, 0, step_at, way), ring_send.at[step_at, way])
-            store(step_at, way, 0).wait()
+        for part_at in range(2):
+            for way, _ in ways(step_at, part_at):
+                wait_bytes(half(owned, 0, part_at), ring_send.at[step_at, way, part_at])
+                store(step_at, way, part_at, 0).wait()
 
 
 def exchange(cov_panel, cov_slab, frames):
@@ -466,9 +474,9 @@
             pltpu.SemaphoreType.DMA((5,)),
             pltpu.SemaphoreType.DMA((15,)),
             pltpu.SemaphoreType.DMA((15,)),
-            pltpu.SemaphoreType.DMA((4, 2)),
-            pltpu.SemaphoreType.DMA((4, 2)),
-            pltpu.SemaphoreType.DMA((4, 2)),
+            pltpu.SemaphoreType.DMA((4, 2, 2)),
+            pltpu.SemaphoreType.DMA((4, 2, 2)),
+            pltpu.SemaphoreType.DMA((4, 2, 2)),
         ],
         compiler_params=pltpu.CompilerParams(
             collective_id=0, has_side_effects=True, vmem_limit_bytes=60 << 20
@@ -480,42 +488,95 @@
 COLS = 512
 
 
-def update_kernel(high, low, rows, wide, slab, sums, heads, out, proj, wide_h, wide_l):
-    @pl.when(pl.program_id(0) == 0)
-    def _():
-        wide_h[...], wide_l[...] = halves(wide[...])
-
-    weights = dot3((high[...], low[...]), halves(rows[...].reshape(COLS, 512)), NT)
-    value = sums[...]
-    for e in range(NC):
-        value = value - exact(heads[e], weights[128 * e : 128 * e + 128, :])
-    proj[...] = value
-    out[...] = slab[...] - dot3((wide_h[...], wide_l[...]), halves(weights), NN)
+def update_kernel(
+    high,
+    low,
+    rows,
+    wide,
+    slab,
+    sums,
+    heads,
+    out,
+    proj,
+    high_v,
+    low_v,
+    rows_v,
+    wide_v,
+    slab_v,
+    out_v,
+    wide_h,
+    wide_l,
+    sem,
+):
+    steps = 1024 // COLS
+    deep = COLS // 128
+    copies = [
+        pltpu.make_async_copy(high, high_v, sem.at[0]),
+        pltpu.make_async_copy(low, low_v, sem.at[1]),
+    ]
+    takes = [
+        pltpu.make_async_copy(
+            rows.at[pl.ds(deep * i, deep)], rows_v.at[pl.ds(deep * i, deep)], sem.at[2 + i]
+        )
+        for i in range(steps)
+    ]
+    whole = pltpu.make_async_copy(wide, wide_v, sem.at[2 + steps])
+    slabs = [
+        pltpu.make_async_copy(
+            slab.at[:, pl.ds(COLS * i, COLS)], slab_v.at[:, pl.ds(COLS * i, COLS)], sem.at[4 + steps + i]
+        )
+        for i in range(steps)
+    ]
+    gives = [
+        pltpu.make_async_copy(
+            out_v.at[:, pl.ds(COLS * i, COLS)], out.at[:, pl.ds(COLS * i, COLS)], sem.at[4 + 2 * steps + i]
+        )
+        for i in range(steps)
+    ]
+    for copy in copies + takes[:1] + [whole] + slabs[:1] + takes[1:] + slabs[1:]:
+        copy.start()
+    for copy in copies:
+        copy.wait()
+    for i in range(steps):
+        at = slice(COLS * i, COLS * i + COLS)
+        takes[i].wait()
+        own = halves(rows_v[deep * i : deep * i + deep].reshape(COLS, 512))
+        weights = dot3((high_v[...], low_v[...]), own, NT)
+        split = halves(weights)
+        across_all = halves(jnp.concatenate([heads[e] for e in range(NC)], axis=1))
+        proj[:, at] = sums[:, at] - dot3(across_all, split, NN)
+        if i == 0:
+            whole.wait()
+            wide_h[...], wide_l[...] = halves(wide_v[...])
+        slabs[i].wait()
+        out_v[:, at] = slab_v[:, at] - dot3((wide_h[...], wide_l[...]), split, NN)
+        gives[i].start()
+    for copy in gives:
+        copy.wait()
 
 
 def update(high, low, rows, wide, cov_slab, sums, heads):
-    once = pl.Buffered(1)
+    any_space = pl.BlockSpec(memory_space=pl.ANY)
+    vmem = pl.BlockSpec(memory_space=pltpu.VMEM)
     return pl.pallas_call(
         update_kernel,
         out_shape=(
             jax.ShapeDtypeStruct((1024, 1024), F32),
             jax.ShapeDtypeStruct((4, 1024), F32),
         ),
-        grid=(1024 // COLS,),
-        in_specs=[
-            pl.BlockSpec((512, 512), lambda i: (0, 0), pipeline_mode=once),
-            pl.BlockSpec((512, 512), lambda i: (0, 0), pipeline_mode=once),
-            pl.BlockSpec((COLS // 128, NXY, 16, 512), lambda i: (i, 0, 0, 0)),
-            pl.BlockSpec((1024, 512), lambda i: (0, 0), pipeline_mode=once),
-            pl.BlockSpec((1024, COLS), lambda i: (0, i)),
-            pl.BlockSpec((4, COLS), lambda i: (0, i)),
-            pl.BlockSpec((NC, 4, 128), lambda i: (0, 0, 0), pipeline_mode=once),
+        in_specs=[any_space] * 5 + [vmem] * 2,
+        out_specs=(any_space, vmem),
+        scratch_shapes=[
+            pltpu.VMEM((512, 512), BF16),
+            pltpu.VMEM((512, 512), BF16),
+            pltpu.VMEM((NZ, NXY, 16, 512), F32),
+            pltpu.VMEM((1024, 512), F32),
+            pltpu.VMEM((1024, 1024), F32),
+            pltpu.VMEM((1024, 1024), F32),
+            pltpu.VMEM((1024, 512), BF16),
+            pltpu.VMEM((1024, 512), BF16),
+            pltpu.SemaphoreType.DMA((4 + 3 * (1024 // COLS),)),
         ],
-        out_specs=(
-            pl.BlockSpec((1024, COLS), lambda i: (0, i)),
-            pl.BlockSpec((4, COLS), lambda i: (0, i)),
-        ),
-        scratch_shapes=[pltpu.VMEM((1024, 512), BF16), pltpu.VMEM((1024, 512), BF16)],
         compiler_params=pltpu.CompilerParams(vmem_limit_bytes=60 << 20),
         name="update",
     )(high, low, rows, wide, cov_slab, sums, heads)

time: 74.7 us -> 71.8 us (0.961)
  Pallas kernels: 73.6 us -> 70.9 us
    pallas_call x1, Pallas kernels: 61.9 us -> 60.1 us  [exchange(): pl.pallas_call(exchange_kernel, out_shape=(jax.ShapeDtypeStruct((512, 512...]
    pallas_call x1, Pallas kernels: 11.7 us -> 10.7 us  [update(): pl.pallas_call(update_kernel, out_shape=(jax.ShapeDtypeStruct((1024, 1024...]
where the time goes in v3:
time: 71.8 us; the launch traced here: 71.5 us
  Pallas kernels  70.9 us (99%)
    pallas_call x1, Pallas kernels, exchange(): pl.pallas_call(exchange_kernel, out_shape=(jax.ShapeDtypeStruct((512, 512...  60.1 us
    pallas_call x1, Pallas kernels, update(): pl.pallas_call(update_kernel, out_shape=(jax.ShapeDtypeStruct((1024, 1024...  10.7 us

profile of v3, /device:TPU:1, one launch (start us, length us, event | category | flops | bytes accessed | tf_op | source)
XLA Modules:
  0.0 71.5 jit_solution(2308580578311667565)
XLA Ops:
  0.6 60.1 %exchange.1 = (bf16[512,512]{1,0:T(8,128)(2,1)}, bf16[512,512]{1,0:T(8,128)(2,1)}, f32[8,8,16,512]{3,2,1,0:T(8,128)}, f32[1024,512]{1,0:T(8,128)}, f32[4,1024]{1,0:T(4,128)}, /*index=5*/f32[4,4,128]{2,1,0:T(4,128)}) custom-call(f32[1024,128]{1,0:T(8,128)} %panel.1, f32[1024,1024]{1,0:T(8,128)} %slab.3, f32[1024,256]{1,0:T(8,128)} %frames.1), custom_call_target="tpu_custom_call" | custom-call | tf_op jit(solution)/shard_map/exchange/pallas_call | solution.py:447
  60.8 10.7 %update.1 = (f32[1024,1024]{1,0:T(8,128)}, f32[4,1024]{1,0:T(4,128)}) custom-call(bf16[512,512]{1,0:T(8,128)(2,1)} %get-tuple-element.8.high, bf16[512,512]{1,0:T(8,128)(2,1)} %get-tuple-element.9.low, f32[8,8,16,512]{3,2,1,0:T(8,128)} %get-tuple-element.10.rows, f32[1024,512]{1,0:T(8,128)} %get-tuple-element.11.wide, f32[1024,1024]{1,0:T(8,128)} %slab.3, ...), custom_call_target="tpu_custom_call" | custom-call | tf_op jit(solution)/shard_map/update/pallas_call | solution.py:561

commit v4 on v3

--- a/solution.py
+++ b/solution.py
@@ -529,9 +529,12 @@
     ]
     gives = [
         pltpu.make_async_copy(
-            out_v.at[:, pl.ds(COLS * i, COLS)], out.at[:, pl.ds(COLS * i, COLS)], sem.at[4 + 2 * steps + i]
+            out_v.at[pl.ds(512 * j, 512), pl.ds(COLS * i, COLS)],
+            out.at[pl.ds(512 * j, 512), pl.ds(COLS * i, COLS)],
+            sem.at[4 + 2 * steps + 2 * i + j],
         )
         for i in range(steps)
+        for j in range(2)
     ]
     for copy in copies + takes[:1] + [whole] + slabs[:1] + takes[1:] + slabs[1:]:
         copy.start()
@@ -549,8 +552,10 @@
             whole.wait()
             wide_h[...], wide_l[...] = halves(wide_v[...])
         slabs[i].wait()
-        out_v[:, at] = slab_v[:, at] - dot3((wide_h[...], wide_l[...]), split, NN)
-        gives[i].start()
+        for j in range(2):
+            up = slice(512 * j, 512 * j + 512)
+            out_v[up, at] = slab_v[up, at] - dot3((wide_h[up, :], wide_l[up, :]), split, NN)
+            gives[2 * i + j].start()
     for copy in gives:
         copy.wait()
 
@@ -575,7 +580,7 @@
             pltpu.VMEM((1024, 1024), F32),
             pltpu.VMEM((1024, 512), BF16),
             pltpu.VMEM((1024, 512), BF16),
-            pltpu.SemaphoreType.DMA((4 + 3 * (1024 // COLS),)),
+            pltpu.SemaphoreType.DMA((4 + 4 * (1024 // COLS),)),
         ],
         compiler_params=pltpu.CompilerParams(vmem_limit_bytes=60 << 20),
         name="update",

time: 71.8 us -> 71.5 us (level)
  no operation moved by 1% of the time
where the time goes in v4:
time: 71.5 us; the launch traced here: 71.2 us
  Pallas kernels  70.6 us (99%)
    pallas_call x1, Pallas kernels, exchange(): pl.pallas_call(exchange_kernel, out_shape=(jax.ShapeDtypeStruct((512, 512...  60.1 us
    pallas_call x1, Pallas kernels, update(): pl.pallas_call(update_kernel, out_shape=(jax.ShapeDtypeStruct((1024, 1024...  10.4 us

profile of v4, /device:TPU:1, one launch (start us, length us, event | category | flops | bytes accessed | tf_op | source)
XLA Modules:
  0.0 71.2 jit_solution(14533361790543815039)
XLA Ops:
  0.6 60.1 %exchange.1 = (bf16[512,512]{1,0:T(8,128)(2,1)}, bf16[512,512]{1,0:T(8,128)(2,1)}, f32[8,8,16,512]{3,2,1,0:T(8,128)}, f32[1024,512]{1,0:T(8,128)}, f32[4,1024]{1,0:T(4,128)}, /*index=5*/f32[4,4,128]{2,1,0:T(4,128)}) custom-call(f32[1024,128]{1,0:T(8,128)} %panel.1, f32[1024,1024]{1,0:T(8,128)} %slab.3, f32[1024,256]{1,0:T(8,128)} %frames.1), custom_call_target="tpu_custom_call" | custom-call | tf_op jit(solution)/shard_map/exchange/pallas_call | solution.py:447
  60.8 10.4 %update.1 = (f32[1024,1024]{1,0:T(8,128)}, f32[4,1024]{1,0:T(4,128)}) custom-call(bf16[512,512]{1,0:T(8,128)(2,1)} %get-tuple-element.8.high, bf16[512,512]{1,0:T(8,128)(2,1)} %get-tuple-element.9.low, f32[8,8,16,512]{3,2,1,0:T(8,128)} %get-tuple-element.10.rows, f32[1024,512]{1,0:T(8,128)} %get-tuple-element.11.wide, f32[1024,1024]{1,0:T(8,128)} %slab.3, ...), custom_call_target="tpu_custom_call" | custom-call | tf_op jit(solution)/shard_map/update/pallas_call | solution.py:566
